TPU v7x, 128 devices: a whole 4x4x4 slice. The times are simulated.
128 devices in a mesh: face: 4 (over y), sub: 32 (over x, z, core).
Axes of the slice: x: 4, y: 4, z: 4, core: 2. Of those that a mesh axis runs over, the one named last changes fastest.
Arguments:
- field: bfloat16 [3, 4, 128, 128, 256], P(None, 'face', 'sub'), may hold values from -6 to 6
- dw_kernel: float32 [9, 256], replicated, may hold values from -2 to 2
- dw_bias: float32 [256], replicated, may hold values from -3 to 3
- zonal_kernel: float32 [7, 256], replicated, may hold values from -2 to 2
- zonal_bias: float32 [256], replicated, may hold values from -3 to 3
- norm_gain: float32 [256], replicated, may hold values from 0.1 to 1.9
- w_in: bfloat16 [256, 768], replicated, may hold values from -0.375 to 0.375
- w_out: bfloat16 [768, 256], replicated, may hold values from -0.21875 to 0.21875
- layer_scale: float32 [256], replicated, may hold values from 0.5 to 1.5
Outputs:
- output: bfloat16 [3, 4, 128, 128, 256], P(None, 'face', 'sub')
All inputs are finite; a program needn't handle non-finite values.
Results may differ from a plain program's by a relative error of at most 0.001.
The roundings to bfloat16 on the way count: a program that leaves them out, or rounds other values in their place, can miss the bound.
Values may be sent and summed in bfloat16 or wider, within the bound.
A program may use at most 64 MiB of HBM per device.

v0:
```python
import jax
import jax.numpy as jnp
from jax import lax
from jax.sharding import PartitionSpec as P

TAPS = 7
DILATION = 4


def extended_2(block, sides, width, periodic):
    for axis, dim in sides:
        count = lax.axis_size(axis)
        forward = [(i, i + 1) for i in range(count - 1)]
        if periodic:
            forward.append((count - 1, 0))
        backward = [(target, source) for source, target in forward]
        low = lax.ppermute(
            lax.slice_in_dim(block, block.shape[dim] - width, None, axis=dim), axis, forward
        )
        high = lax.ppermute(lax.slice_in_dim(block, 0, width, axis=dim), axis, backward)
        block = jnp.concatenate([low, block, high], axis=dim)
    return block


def cut_along(value, dim, size):
    before, after = (value.shape[:dim], value.shape[dim + 1 :])
    return jnp.moveaxis(value.reshape(*before, size, -1, *after), dim, 0)


def sum_at_owner(value, axis, dim):
    parts = cut_along(value, dim, lax.axis_size(axis))
    arrived = lax.all_to_all(parts, axis, split_axis=0, concat_axis=0, tiled=True)
    return arrived.astype(jnp.float32).sum(axis=0)


def joined_along(parts, dim):
    dims = list(parts.shape[1:])
    dims[dim] *= parts.shape[0]
    return jnp.moveaxis(parts, 0, dim).reshape(dims)


def copy_for_each(value, axis):
    size = lax.axis_size(axis)
    return lax.all_to_all(
        jnp.broadcast_to(value[None], (size, *value.shape)), axis, 0, 0, tiled=True
    )


def gathered_copies(value, axis, dim):
    return joined_along(copy_for_each(value, axis), dim)


def cycle_place(facet, column, row_pos, side):
    cycle = (facet + 2) * side - column - row_pos - 1
    along = jnp.where(
        facet == 0,
        column + cycle - side,
        jnp.where((facet == 1) & (cycle < 2 * side), column + cycle - 2 * side, column),
    )
    arc_len = jnp.minimum(jnp.minimum(cycle, side), 4 * side - cycle)
    return (cycle, along, arc_len)


def cycle_cell(cycle, along, side):
    north = (cycle < 2 * side) & (along >= cycle - side)
    middle = jnp.logical_not(north) & (along < 3 * side - cycle)
    facet = jnp.where(north, jnp.int32(0), jnp.where(middle, jnp.int32(1), jnp.int32(2)))
    column = jnp.where(
        north,
        along - cycle + side,
        jnp.where(middle & (cycle < 2 * side), along + 2 * side - cycle, along),
    )
    row_pos = (facet + 2) * side - 1 - cycle - column
    return (facet, column, row_pos)


def take_row(segment_block, permutation):
    return jnp.take(segment_block, permutation, axis=2)


def reorder(values, order):
    return jax.vmap(take_row, in_axes=(1, 0), out_axes=1)(values, order)


def shards(
    field, dw_kernel, dw_bias, zonal_kernel, zonal_bias, norm_gain, w_in, w_out, layer_scale
):
    local_field = field[:, 0]
    rows_here = local_field.shape[1]
    side_cells = local_field.shape[2]
    channels = local_field.shape[3]
    edge_index = side_cells - 1
    sub_count = lax.axis_size("sub")
    quad_total = lax.axis_size("face")
    sub_index = lax.axis_index("sub")
    quad_index = lax.axis_index("face")
    row_start = sub_index * rows_here
    side_pair = jnp.stack([local_field[1, :, 0], local_field[2, :, edge_index]])
    beside_all = extended_2(side_pair, (("face", 0),), 1, True)
    last_lines = jnp.where(
        sub_index == sub_count - 1, local_field[:, rows_here - 1], jnp.zeros_like(local_field[:, 0])
    )
    first_lines = jnp.where(sub_index == 0, local_field[:, 0], jnp.zeros_like(local_field[:, 0]))
    rim_lines = jnp.swapaxes(jnp.concatenate([last_lines, first_lines], 0), 0, 1)
    pieces = sum_at_owner(rim_lines.astype(jnp.float32).astype(jnp.bfloat16), "sub", 0).astype(
        jnp.bfloat16
    )
    strips = jnp.stack(
        [
            pieces[:, 0],
            pieces[:, 1],
            local_field[2, :, 0],
            pieces[:, 5],
            local_field[0, :, edge_index],
            pieces[:, 3],
        ]
    )
    near = extended_2(strips, (("face", 0),), 3, True)
    wanted = jnp.stack([near[10], pieces[:, 2], near[11], near[1], near[2], pieces[:, 4]])
    lines = gathered_copies(wanted, "sub", 1)
    left_slice = near[0]
    right_slice = near[9]
    face_top = lines[0:3]
    face_bottom = lines[3:6]
    left_side = jnp.stack([local_field[1, :, edge_index], beside_all[0], left_slice])
    right_side = jnp.stack([right_slice, local_field[0, :, 0], beside_all[3]])
    widened = jnp.concatenate([left_side[:, :, None], local_field, right_side[:, :, None]], 2)
    extended = extended_2(widened, (("sub", 1),), 1, False)
    corner = jnp.zeros((3, 1, channels), local_field.dtype)
    face_top = jnp.concatenate([corner, face_top, corner], 1)
    face_bottom = jnp.concatenate([corner, face_bottom, corner], 1)
    first_row = jnp.where(sub_index == 0, face_top, extended[:, 0])
    final_row = jnp.where(sub_index == sub_count - 1, face_bottom, extended[:, rows_here + 1])
    padded = jnp.concatenate(
        [first_row[:, None], extended[:, 1 : rows_here + 1], final_row[:, None]], 1
    )
    total = jnp.zeros((3, rows_here, side_cells, channels), jnp.float32) + dw_bias
    for i in range(3):
        for j in range(3):
            total = total + dw_kernel[3 * i + j] * padded[
                :, i : i + rows_here, j : j + side_cells
            ].astype(jnp.float32)
    mixed = total.astype(jnp.bfloat16)
    shard_count = quad_total * sub_count
    shard_id = quad_index * sub_count + sub_index
    blocks = side_cells // shard_count
    row_ids = row_start + lax.broadcasted_iota(jnp.int32, (rows_here, shard_count), 0)
    shard_ids = lax.broadcasted_iota(jnp.int32, (rows_here, shard_count), 1)
    order = (-row_ids - 1 - shard_ids) % shard_count
    sending = reorder(mixed.reshape(3, rows_here, blocks, shard_count, channels), order)
    arrived = lax.all_to_all(sending, ("face", "sub"), split_axis=3, concat_axis=3, tiled=True)
    buffer = arrived.reshape(3, rows_here, blocks, quad_total, sub_count, channels)
    shape_out = (3, rows_here, blocks, quad_total, sub_count)
    facet = lax.broadcasted_iota(jnp.int32, shape_out, 0)
    row_local = lax.broadcasted_iota(jnp.int32, shape_out, 1)
    block_ids = lax.broadcasted_iota(jnp.int32, shape_out, 2)
    quad_out = lax.broadcasted_iota(jnp.int32, shape_out, 3)
    sub_source = lax.broadcasted_iota(jnp.int32, shape_out, 4)
    row_pos = sub_source * rows_here + row_local
    residue = (-row_pos - 1 - shard_id) % shard_count
    column = shard_count * block_ids + residue
    cycle, along, arc_len = cycle_place(facet, column, row_pos, side_cells)
    place = quad_out * arc_len + along
    flat = buffer.reshape(-1, channels)
    half = TAPS // 2
    accum = jnp.zeros(shape_out + (channels,), jnp.float32) + zonal_bias
    for k in range(TAPS):
        moved = (place + DILATION * (k - half)) % (4 * arc_len)
        quad_new = moved // arc_len
        along_new = moved % arc_len
        facet_new, column_new, row_new = cycle_cell(cycle, along_new, side_cells)
        index = (
            ((facet_new * rows_here + row_new % rows_here) * blocks + column_new // shard_count)
            * quad_total
            + quad_new
        ) * sub_count + row_new // rows_here
        gathered = jnp.take(flat, index.reshape(-1), axis=0).reshape(shape_out + (channels,))
        accum = accum + zonal_kernel[k] * gathered.astype(jnp.float32)
    zonal = accum.astype(jnp.bfloat16)
    returned = lax.all_to_all(
        zonal.reshape(3, rows_here, blocks, shard_count, channels),
        ("face", "sub"),
        split_axis=3,
        concat_axis=3,
        tiled=True,
    )
    restored = reorder(returned, order).reshape(3, rows_here, side_cells, channels)

    def finish(pair):
        zonal_face, input_face = pair
        values = zonal_face.reshape(-1, channels).astype(jnp.float32)
        mean = jnp.mean(values, -1, keepdims=True)
        spread = jnp.mean(jnp.square(values - mean), -1, keepdims=True)
        normed = ((values - mean) * lax.rsqrt(spread + 1e-06) * norm_gain).astype(jnp.bfloat16)
        hidden = jax.nn.gelu(
            jnp.dot(normed, w_in, preferred_element_type=jnp.float32), approximate=False
        ).astype(jnp.bfloat16)
        branch = jnp.dot(hidden, w_out, preferred_element_type=jnp.float32)
        source = input_face.reshape(-1, channels).astype(jnp.float32)
        result = (source + layer_scale * branch).astype(jnp.bfloat16)
        return result.reshape(rows_here, side_cells, channels)

    output = lax.map(finish, (restored, local_field))
    return output[:, None]


def solution(mesh):
    in_specs = (P(None, "face", "sub", None, None), P(), P(), P(), P(), P(), P(), P(), P())
    out_specs = P(None, "face", "sub", None, None)
    return jax.shard_map(shards, mesh=mesh, in_specs=in_specs, out_specs=out_specs, check_vma=False)
```

profile of v0, /device:TPU:1, one launch (start us, length us, event | category | flops | bytes accessed | tf_op | source)
XLA Modules:
  0.0 164.4 jit_solution(5760792183229900761)
XLA Ops:
  2.1 9.4 %all-to-all-start = ((bf16[32,4,6,256]{3,1,2,0:T(4,128)(2,1)}), bf16[32,4,6,256]{3,1,2,0:T(4,128)(2,1)S(1)}, u32[]{:S(2)}, u32[]{:S(2)}) async-start(bf16[32,4,6,256]{3,1,2,0:T(4,128)(2,1)} %copy.316), calls=%async_computation | async-start | bytes 786432 | tf_op jit(solution)/shard_map/all_to_all | solution.py:32
  11.6 2.8 %collective-permute-start.3 = (bf16[1,4,256]{2,1,0:T(4,128)(2,1)S(1)}, bf16[1,4,256]{2,1,0:T(4,128)(2,1)S(1)}, u32[]{:S(2)}, u32[]{:S(2)}) collective-permute-start(bf16[1,4,256]{2,1,0:T(4,128)(2,1)S(1)} %bitcast.200), channel_id=1, source_target_pairs={{32,0},{64,32},{96,64},{0,96},{33,1},{65,33},{97,65},{1,97},{34,2}... | collective-permute-start | bytes 6152 | tf_op jit(solution)/shard_map/ppermute | solution.py:20
  15.7 6.1 %all-to-all-done = bf16[32,4,6,256]{3,1,2,0:T(4,128)(2,1)S(1)} async-done(((bf16[32,4,6,256]{3,1,2,0:T(4,128)(2,1)}), bf16[32,4,6,256]{3,1,2,0:T(4,128)(2,1)S(1)}, u32[]{:S(2)}, u32[]{:S(2)}) %all-to-all-start) | async-done | bytes 393248 | tf_op jit(solution)/shard_map/all_to_all | solution.py:32
  22.0 2.8 %collective-permute-start = (bf16[3,4,256]{2,1,0:T(4,128)(2,1)S(1)}, bf16[3,4,256]{2,1,0:T(4,128)(2,1)S(1)}, u32[]{:S(2)}, u32[]{:S(2)}) collective-permute-start(bf16[3,4,256]{2,1,0:T(4,128)(2,1)S(1)} %pad_maximum_fusion.10), channel_id=1, source_target_pairs={{32,0},{64,32},{96,64},{0,96},{33,1},{65,33},{97,65},{1,97},{34,2}... | collective-permute-start | bytes 18440 | tf_op jit(solution)/shard_map/ppermute | solution.py:20
  25.6 3.0 %collective-permute-done.1 = bf16[3,4,256]{2,1,0:T(4,128)(2,1)S(1)} collective-permute-done((bf16[3,4,256]{2,1,0:T(4,128)(2,1)S(1)}, bf16[3,4,256]{2,1,0:T(4,128)(2,1)S(1)}, u32[]{:S(2)}, u32[]{:S(2)}) %collective-permute-start.1) | collective-permute-done | bytes 6176 | tf_op jit(solution)/shard_map/ppermute | solution.py:17
  29.5 5.0 %all-to-all-start.1 = ((bf16[32,6,4,256]{3,2,1,0:T(4,128)(2,1)}), bf16[32,6,4,256]{3,2,1,0:T(4,128)(2,1)S(1)}, u32[]{:S(2)}, u32[]{:S(2)}) async-start(bf16[32,6,4,256]{3,2,1,0:T(4,128)(2,1)} %broadcast_in_dim.92), calls=%async_computation.1 | async-start | bytes 786432 | tf_op jit(solution)/shard_map/all_to_all | solution.py:44
  34.8 3.5 %collective-permute-start.4 = (bf16[3,1,130,256]{3,2,1,0:T(8,128)(2,1)S(1)}, bf16[3,1,130,256]{3,2,1,0:T(8,128)(2,1)S(1)}, u32[]{:S(2)}, u32[]{:S(2)}) collective-permute-start(bf16[3,1,130,256]{3,2,1,0:T(8,128)(2,1)S(1)} %get-tuple-element.174), channel_id=1, source_target_pairs={{0,1},{1,2},{2,3},{3,4},{4,5},{5,6},{6,7},{7,8},{8,9},{9,10},{10,1... | collective-permute-start | bytes 599048 | tf_op jit(solution)/shard_map/ppermute | solution.py:17
  38.4 1.9 %collective-permute-start.5 = (bf16[3,1,130,256]{3,2,1,0:T(8,128)(2,1)S(1)}, bf16[3,1,130,256]{3,2,1,0:T(8,128)(2,1)S(1)}, u32[]{:S(2)}, u32[]{:S(2)}) collective-permute-start(bf16[3,1,130,256]{3,2,1,0:T(8,128)(2,1)S(1)} %get-tuple-element.175), channel_id=1, source_target_pairs={{1,0},{2,1},{3,2},{4,3},{5,4},{6,5},{7,6},{8,7},{9,8},{10,9},{11,1... | collective-permute-start | bytes 599048 | tf_op jit(solution)/shard_map/ppermute | solution.py:20
  40.3 4.5 %all-to-all-done.1 = bf16[32,6,4,256]{3,2,1,0:T(4,128)(2,1)S(1)} async-done(((bf16[32,6,4,256]{3,2,1,0:T(4,128)(2,1)}), bf16[32,6,4,256]{3,2,1,0:T(4,128)(2,1)S(1)}, u32[]{:S(2)}, u32[]{:S(2)}) %all-to-all-start.1) | async-done | bytes 393248 | tf_op jit(solution)/shard_map/all_to_all | solution.py:44
  46.5 2.2 %fusion.86 = bf16[4,3,128,256]{3,2,0,1:T(8,128)(2,1)S(1)} fusion(bf16[3,5,130,256]{3,2,1,0:T(8,128)(2,1)S(1)} %get-tuple-element.173, f32[256]{0:T(256)S(1)} %bitcast.197, f32[256]{0:T(256)S(1)} %bitcast.198, f32[256]{0:T(256)S(1)} %bitcast.191, bf16[3,4,1,256]{3,2,1,0:T(2,128)(2,1)S(1)} %copy.320, bf16[3,4,128,256]{3,2,1,0:T(8,128)(2,1)S(1)} %bitcast.164, ...), kind=kLoop, calls=%fused_computation.134 | loop fusion | flops 13369344 | bytes 6313984 | tf_op jit(solution)/shard_map/vmap(jit(_take))/transpose | solution.py:78
  49.4 2.8 %gather_fusion = bf16[512,3,256]{2,1,0:T(4,128)(2,1)S(1)} fusion(bf16[4,3,128,256]{3,1,2,0:T(4,128)(2,1)S(1)} %copy.325, s32[512]{0:T(512)S(1)} %fusion.195), kind=kCustom, calls=%fused_computation.clone | custom fusion | bytes 1576960 | tf_op jit(solution)/shard_map/vmap(jit(_take))/gather | solution.py:78
  52.2 1.7 %fusion.85 = bf16[3,4,1,128,256]{4,1,2,0,3:T(4,128)(2,1)} fusion(bf16[4,128,3,256]{3,2,1,0:T(4,128)(2,1)S(1)} %bitcast.168, pred[4,128]{0,1:T(8,128)(4,1)S(1)} %copy.315), kind=kLoop, calls=%fused_computation.126 | loop fusion | flops 393216 | bytes 1573376 | tf_op jit(solution)/shard_map/vmap()/transpose | solution.py:82
  53.9 7.8 %all-to-all-start.2 = ((bf16[3,4,1,128,256]{4,1,2,0,3:T(4,128)(2,1)}), bf16[3,4,1,128,256]{4,1,2,0,3:T(4,128)(2,1)S(1)}, u32[]{:S(2)}, u32[]{:S(2)}) async-start(bf16[3,4,1,128,256]{4,1,2,0,3:T(4,128)(2,1)} %fusion.85), calls=%async_computation.2 | async-start | bytes 1572864 | tf_op jit(solution)/shard_map/all_to_all | solution.py:151
  61.8 1.6 compare_and_fusion.5
  63.5 14.5 %all-to-all-done.2 = bf16[3,4,1,128,256]{4,1,2,0,3:T(4,128)(2,1)S(1)} async-done(((bf16[3,4,1,128,256]{4,1,2,0,3:T(4,128)(2,1)}), bf16[3,4,1,128,256]{4,1,2,0,3:T(4,128)(2,1)S(1)}, u32[]{:S(2)}, u32[]{:S(2)}) %all-to-all-start.2) | async-done | bytes 786464 | tf_op jit(solution)/shard_map/all_to_all | solution.py:151
  78.1 5.4 %gather_fusion.2 = bf16[1536,256]{1,0:T(8,128)(2,1)} fusion(bf16[1536,256]{1,0:T(8,128)(2,1)S(1)} %bitcast.153, s32[2048]{0:T(1024)S(1)} %get-tuple-element.227), kind=kCustom, calls=%fused_computation.3.clone | custom fusion | bytes 1579008 | tf_op jit(solution)/shard_map/jit(_take)/gather | solution.py:177
  83.5 5.3 %gather_fusion.3 = bf16[1536,256]{1,0:T(8,128)(2,1)} fusion(bf16[1536,256]{1,0:T(8,128)(2,1)S(1)} %bitcast.154, s32[2048]{0:T(1024)S(1)} %get-tuple-element.226), kind=kCustom, calls=%fused_computation.4.clone | custom fusion | bytes 1579008 | tf_op jit(solution)/shard_map/jit(_take)/gather | solution.py:177
  88.8 5.4 %gather_fusion.4 = bf16[1536,256]{1,0:T(8,128)(2,1)} fusion(bf16[1536,256]{1,0:T(8,128)(2,1)S(1)} %bitcast.155, s32[2048]{0:T(1024)S(1)} %get-tuple-element.225), kind=kCustom, calls=%fused_computation.5.clone | custom fusion | bytes 1579008 | tf_op jit(solution)/shard_map/jit(_take)/gather | solution.py:177
  94.2 5.3 %gather_fusion.5 = bf16[1536,256]{1,0:T(8,128)(2,1)} fusion(bf16[1536,256]{1,0:T(8,128)(2,1)S(1)} %bitcast.156, s32[2048]{0:T(1024)S(1)} %get-tuple-element.224), kind=kCustom, calls=%fused_computation.6.clone | custom fusion | bytes 1579008 | tf_op jit(solution)/shard_map/jit(_take)/gather | solution.py:177
  99.5 5.4 %gather_fusion.6 = bf16[1536,256]{1,0:T(8,128)(2,1)} fusion(bf16[1536,256]{1,0:T(8,128)(2,1)S(1)} %bitcast.157, s32[2048]{0:T(1024)S(1)} %get-tuple-element.223), kind=kCustom, calls=%fused_computation.7.clone | custom fusion | bytes 1579008 | tf_op jit(solution)/shard_map/jit(_take)/gather | solution.py:177
  104.9 4.8 %gather_fusion.1 = bf16[1536,256]{1,0:T(8,128)(2,1)S(1)} fusion(bf16[1536,256]{1,0:T(8,128)(2,1)S(1)} %bitcast.158, s32[2048]{0:T(1024)S(1)} %pad_clamp_fusion.6), kind=kCustom, calls=%fused_computation.1.clone | custom fusion | bytes 1579008 | tf_op jit(solution)/shard_map/jit(_take)/gather | solution.py:177
  109.7 4.8 %gather_fusion.7 = bf16[1536,256]{1,0:T(8,128)(2,1)S(1)} fusion(bf16[1536,256]{1,0:T(8,128)(2,1)S(1)} %bitcast.159, s32[2048]{0:T(1024)S(1)} %get-tuple-element.222), kind=kCustom, calls=%fused_computation.8.clone | custom fusion | bytes 1579008 | tf_op jit(solution)/shard_map/jit(_take)/gather | solution.py:177
  114.4 1.5 broadcast_select_fusion.5
  119.7 1.1 fusion.77
  120.9 1.5 copy.328
  122.4 4.7 %all-to-all-start.3 = ((bf16[3,4,1,128,256]{4,1,2,0,3:T(4,128)(2,1)}), bf16[3,4,1,128,256]{4,1,2,0,3:T(4,128)(2,1)S(1)}, u32[]{:S(2)}, u32[]{:S(2)}) async-start(bf16[3,4,1,128,256]{4,1,2,0,3:T(4,128)(2,1)} %copy.328), calls=%async_computation.3 | async-start | bytes 1572864 | tf_op jit(solution)/shard_map/all_to_all | solution.py:180
  127.1 16.4 %all-to-all-done.3 = bf16[3,4,1,128,256]{4,1,2,0,3:T(4,128)(2,1)S(1)} async-done(((bf16[3,4,1,128,256]{4,1,2,0,3:T(4,128)(2,1)}), bf16[3,4,1,128,256]{4,1,2,0,3:T(4,128)(2,1)S(1)}, u32[]{:S(2)}, u32[]{:S(2)}) %all-to-all-start.3) | async-done | bytes 786464 | tf_op jit(solution)/shard_map/all_to_all | solution.py:180
  143.9 2.8 %gather_fusion.8 = bf16[512,3,256]{2,1,0:T(4,128)(2,1)S(1)} fusion(bf16[4,3,128,256]{3,1,2,0:T(4,128)(2,1)S(1)} %bitcast.169, s32[512]{0:T(512)S(1)} %fusion.195), kind=kCustom, calls=%fused_computation.2.clone | custom fusion | bytes 1576960 | tf_op jit(solution)/shard_map/vmap(jit(_take))/gather | solution.py:78
  147.4 17.1 %while.10 = (s32[]{:T(128)}, bf16[3,4,128,256]{3,2,1,0:T(8,128)(2,1)}, bf16[3,4,128,256]{3,2,1,0:T(8,128)(2,1)S(1)}, f32[256]{0:T(256)S(1)}, bf16[3,4,128,256]{3...) while((s32[]{:T(128)}, ...), condition=%wide.region_4.7_spmd, body=%wide.region_1.6_spmd.sunk | while | flops 430178816 | bytes 6838949 | solution.py:203
  148.5 3.8 %fusion.214 = bf16[512,256]{1,0:T(8,128)(2,1)S(1)} fusion(bf16[768,256]{1,0:T(8,128)(2,1)S(1)} %copy-done.11, bf16[512,256]{1,0:T(8,128)(2,1)S(1)} %fusion.213, bf16[256,768]{1,0:T(8,128)(2,1)S(1)} %copy-done.10, bf16[512,256]{1,0:T(8,128)(2,1)S(1)} %bitcast.167, f32[256]{0:T(256)S(1)} %get-tuple-element.302), kind=kOutput, calls=%fused_computation.30.clone.1 | convolution fusion | flops 428736512 | bytes 1573888 | tf_op jit(solution)/shard_map/while/body/eval_jaxpr/dot_general | solution.py:198
  154.2 3.8 %fusion.214 = bf16[512,256]{1,0:T(8,128)(2,1)S(1)} fusion(bf16[768,256]{1,0:T(8,128)(2,1)S(1)} %copy-done.11, bf16[512,256]{1,0:T(8,128)(2,1)S(1)} %fusion.213, bf16[256,768]{1,0:T(8,128)(2,1)S(1)} %copy-done.10, bf16[512,256]{1,0:T(8,128)(2,1)S(1)} %bitcast.167, f32[256]{0:T(256)S(1)} %get-tuple-element.302), kind=kOutput, calls=%fused_computation.30.clone.1 | convolution fusion | flops 428736512 | bytes 1573888 | tf_op jit(solution)/shard_map/while/body/eval_jaxpr/dot_general | solution.py:198
  159.9 3.8 %fusion.214 = bf16[512,256]{1,0:T(8,128)(2,1)S(1)} fusion(bf16[768,256]{1,0:T(8,128)(2,1)S(1)} %copy-done.11, bf16[512,256]{1,0:T(8,128)(2,1)S(1)} %fusion.213, bf16[256,768]{1,0:T(8,128)(2,1)S(1)} %copy-done.10, bf16[512,256]{1,0:T(8,128)(2,1)S(1)} %bitcast.167, f32[256]{0:T(256)S(1)} %get-tuple-element.302), kind=kOutput, calls=%fused_computation.30.clone.1 | convolution fusion | flops 428736512 | bytes 1573888 | tf_op jit(solution)/shard_map/while/body/eval_jaxpr/dot_general | solution.py:198
  (132 shorter events, 18.2 us)
Async XLA Ops:
  1.1 10.4 %copy-start = (bf16[3,1,4,128,256]{4,3,2,1,0:T(8,128)(2,1)S(1)}, bf16[3,1,4,128,256]{4,3,2,1,0:T(8,128)(2,1)}, u32[]{:S(2)}) copy-start(bf16[3,1,4,128,256]{4,3,2,1,0:T(8,128)(2,1)} %param.15) | copy-start | bytes 2359300
  1.1 13.4 %copy-start.7 = (f32[9,256]{1,0:T(8,128)S(1)}, f32[9,256]{1,0:T(8,128)}, u32[]{:S(2)}) copy-start(f32[9,256]{1,0:T(8,128)} %param.16) | copy-start | bytes 27652
  2.1 19.7 %all-to-all-start = ((bf16[32,4,6,256]{3,1,2,0:T(4,128)(2,1)}), bf16[32,4,6,256]{3,1,2,0:T(4,128)(2,1)S(1)}, u32[]{:S(2)}, u32[]{:S(2)}) async-start(bf16[32,4,6,256]{3,1,2,0:T(4,128)(2,1)} %copy.316), calls=%async_computation | async-start | bytes 786432 | tf_op jit(solution)/shard_map/all_to_all | solution.py:32
  11.6 23.0 %collective-permute-start.3 = (bf16[1,4,256]{2,1,0:T(4,128)(2,1)S(1)}, bf16[1,4,256]{2,1,0:T(4,128)(2,1)S(1)}, u32[]{:S(2)}, u32[]{:S(2)}) collective-permute-start(bf16[1,4,256]{2,1,0:T(4,128)(2,1)S(1)} %bitcast.200), channel_id=1, source_target_pairs={{32,0},{64,32},{96,64},{0,96},{33,1},{65,33},{97,65},{1,97},{34,2}... | collective-permute-start | bytes 6152 | tf_op jit(solution)/shard_map/ppermute | solution.py:20
  14.4 20.3 %collective-permute-start.2 = (bf16[1,4,256]{2,1,0:T(4,128)(2,1)S(1)}, bf16[1,4,256]{2,1,0:T(4,128)(2,1)S(1)}, u32[]{:S(2)}, u32[]{:S(2)}) collective-permute-start(bf16[1,4,256]{2,1,0:T(4,128)(2,1)S(1)} %bitcast.199), channel_id=1, source_target_pairs={{0,32},{32,64},{64,96},{96,0},{1,33},{33,65},{65,97},{97,1},{2,34}... | collective-permute-start | bytes 6152 | tf_op jit(solution)/shard_map/ppermute | solution.py:17
  22.0 3.6 %collective-permute-start = (bf16[3,4,256]{2,1,0:T(4,128)(2,1)S(1)}, bf16[3,4,256]{2,1,0:T(4,128)(2,1)S(1)}, u32[]{:S(2)}, u32[]{:S(2)}) collective-permute-start(bf16[3,4,256]{2,1,0:T(4,128)(2,1)S(1)} %pad_maximum_fusion.10), channel_id=1, source_target_pairs={{32,0},{64,32},{96,64},{0,96},{33,1},{65,33},{97,65},{1,97},{34,2}... | collective-permute-start | bytes 18440 | tf_op jit(solution)/shard_map/ppermute | solution.py:20
  24.8 3.8 %collective-permute-start.1 = (bf16[3,4,256]{2,1,0:T(4,128)(2,1)S(1)}, bf16[3,4,256]{2,1,0:T(4,128)(2,1)S(1)}, u32[]{:S(2)}, u32[]{:S(2)}) collective-permute-start(bf16[3,4,256]{2,1,0:T(4,128)(2,1)S(1)} %pad_maximum_fusion.11), channel_id=1, source_target_pairs={{0,32},{32,64},{64,96},{96,0},{1,33},{33,65},{65,97},{97,1},{2,34}... | collective-permute-start | bytes 18440 | tf_op jit(solution)/shard_map/ppermute | solution.py:17
  29.5 15.3 %all-to-all-start.1 = ((bf16[32,6,4,256]{3,2,1,0:T(4,128)(2,1)}), bf16[32,6,4,256]{3,2,1,0:T(4,128)(2,1)S(1)}, u32[]{:S(2)}, u32[]{:S(2)}) async-start(bf16[32,6,4,256]{3,2,1,0:T(4,128)(2,1)} %broadcast_in_dim.92), calls=%async_computation.1 | async-start | bytes 786432 | tf_op jit(solution)/shard_map/all_to_all | solution.py:44
  34.8 10.3 %collective-permute-start.4 = (bf16[3,1,130,256]{3,2,1,0:T(8,128)(2,1)S(1)}, bf16[3,1,130,256]{3,2,1,0:T(8,128)(2,1)S(1)}, u32[]{:S(2)}, u32[]{:S(2)}) collective-permute-start(bf16[3,1,130,256]{3,2,1,0:T(8,128)(2,1)S(1)} %get-tuple-element.174), channel_id=1, source_target_pairs={{0,1},{1,2},{2,3},{3,4},{4,5},{5,6},{6,7},{7,8},{8,9},{9,10},{10,1... | collective-permute-start | bytes 599048 | tf_op jit(solution)/shard_map/ppermute | solution.py:17
  38.4 7.2 %collective-permute-start.5 = (bf16[3,1,130,256]{3,2,1,0:T(8,128)(2,1)S(1)}, bf16[3,1,130,256]{3,2,1,0:T(8,128)(2,1)S(1)}, u32[]{:S(2)}, u32[]{:S(2)}) collective-permute-start(bf16[3,1,130,256]{3,2,1,0:T(8,128)(2,1)S(1)} %get-tuple-element.175), channel_id=1, source_target_pairs={{1,0},{2,1},{3,2},{4,3},{5,4},{6,5},{7,6},{8,7},{9,8},{10,9},{11,1... | collective-permute-start | bytes 599048 | tf_op jit(solution)/shard_map/ppermute | solution.py:20
  45.8 0.7 copy-start.8
  53.9 9.5 %copy-start.6 = (f32[7,256]{1,0:T(8,128)S(1)}, f32[7,256]{1,0:T(8,128)}, u32[]{:S(2)}) copy-start(f32[7,256]{1,0:T(8,128)} %param.18) | copy-start | bytes 21508
  53.9 24.1 %all-to-all-start.2 = ((bf16[3,4,1,128,256]{4,1,2,0,3:T(4,128)(2,1)}), bf16[3,4,1,128,256]{4,1,2,0,3:T(4,128)(2,1)S(1)}, u32[]{:S(2)}, u32[]{:S(2)}) async-start(bf16[3,4,1,128,256]{4,1,2,0,3:T(4,128)(2,1)} %fusion.85), calls=%async_computation.2 | async-start | bytes 1572864 | tf_op jit(solution)/shard_map/all_to_all | solution.py:151
  114.4 1.5 copy-start.4
  115.9 1.1 copy-start.2
  116.2 1.2 copy-start.3
  117.3 1.2 copy-start.1
  119.0 0.7 copy-start.9
  122.4 21.1 %all-to-all-start.3 = ((bf16[3,4,1,128,256]{4,1,2,0,3:T(4,128)(2,1)}), bf16[3,4,1,128,256]{4,1,2,0,3:T(4,128)(2,1)S(1)}, u32[]{:S(2)}, u32[]{:S(2)}) async-start(bf16[3,4,1,128,256]{4,1,2,0,3:T(4,128)(2,1)} %copy.328), calls=%async_computation.3 | async-start | bytes 1572864 | tf_op jit(solution)/shard_map/all_to_all | solution.py:180
  146.7 0.7 copy-start.5
  146.7 0.7 copy-start.12
  147.4 1.0 copy-start.10
  147.4 1.1 copy-start.11
  153.1 1.0 copy-start.10
  153.1 1.1 copy-start.11
  158.8 1.0 copy-start.10
  158.8 1.1 copy-start.11
where the time goes:
time: 165 us; the launch traced here: 164 us
  local copies, waits for them, and re-layouts  54.2 us (33%)
  waiting for transfers between devices  45.5 us (28%)
  starting transfers between devices  38.1 us (23%)
  other arithmetic  14.4 us (9%)
  matrix products  11.5 us (7%)
    gather x7, local copies, waits for them, and re-layouts, shards(): jnp.take(flat, index.reshape(-1), axis=0).reshape(shape_out + (channels,))  36.3 us
    all_to_all x1, waiting for transfers between devices, shards(): lax.all_to_all(zonal.reshape(3, rows_here, blocks, shard_count, channels)...  16.4 us
    all_to_all x1, waiting for transfers between devices, shards(): lax.all_to_all(sending, ('face', 'sub'), split_axis=3, concat_axis=3, til...  14.5 us
    dot_general x3, matrix products, finish(): branch = jnp.dot(hidden, w_out, preferred_element_type=jnp.float32)  11.5 us
    all_to_all x1, starting transfers between devices, sum_at_owner(): lax.all_to_all(parts, axis, split_axis=0, concat_axis=0, tiled=True)  9.42 us
    all_to_all x1, starting transfers between devices, shards(): lax.all_to_all(sending, ('face', 'sub'), split_axis=3, concat_axis=3, til...  7.84 us
    ppermute x3, starting transfers between devices, extended_2(): lax.ppermute(lax.slice_in_dim(block, 0, width, axis=dim), axis, backward)  7.53 us
    all_to_all x1, waiting for transfers between devices, sum_at_owner(): lax.all_to_all(parts, axis, split_axis=0, concat_axis=0, tiled=True)  6.07 us
  transfers between devices with their start and end apart: 10, of which 7 were waited for; matrix products, arithmetic and copies ran while one was open for 3% of the time, Pallas kernels for 0%

commit v1 on v0

--- a/solution.py
+++ b/solution.py
@@ -148,7 +148,15 @@
     shard_ids = lax.broadcasted_iota(jnp.int32, (rows_here, shard_count), 1)
     order = (-row_ids - 1 - shard_ids) % shard_count
     sending = reorder(mixed.reshape(3, rows_here, blocks, shard_count, channels), order)
-    arrived = lax.all_to_all(sending, ("face", "sub"), split_axis=3, concat_axis=3, tiled=True)
+    arrived = jnp.concatenate(
+        lax.all_to_all(
+            jnp.stack(jnp.split(sending, lax.axis_size(("face", "sub")), axis=3)),
+            ("face", "sub"),
+            0,
+            0,
+        ),
+        axis=3,
+    )
     buffer = arrived.reshape(3, rows_here, blocks, quad_total, sub_count, channels)
     shape_out = (3, rows_here, blocks, quad_total, sub_count)
     facet = lax.broadcasted_iota(jnp.int32, shape_out, 0)

time: 165 us -> 241 us (1.46)
  local copies, waits for them, and re-layouts: 54.2 us -> 131 us
    unnamed x31 -> x158, local copies, waits for them, and re-layouts: 2.99 us -> 78.8 us
  transfers between devices with their start and end apart: 10 -> 10, of which waited for: 7 -> 7; matrix products, arithmetic and copies ran while one was open for 3% -> 2% of each run, Pallas kernels for 0% -> 0%
where the time goes in v1:
time: 241 us; the launch traced here: 240 us
  local copies, waits for them, and re-layouts  131 us (54%)
  waiting for transfers between devices  45.5 us (19%)
  starting transfers between devices  38.1 us (16%)
  other arithmetic  13.5 us (6%)
  matrix products  11.5 us (5%)
    unnamed x158, local copies, waits for them, and re-layouts  78.8 us
    gather x7, local copies, waits for them, and re-layouts, shards(): jnp.take(flat, index.reshape(-1), axis=0).reshape(shape_out + (channels,))  36.3 us
    all_to_all x1, waiting for transfers between devices, shards(): lax.all_to_all(zonal.reshape(3, rows_here, blocks, shard_count, channels)...  16.4 us
    all_to_all x1, waiting for transfers between devices, shards(): lax.all_to_all(jnp.stack(jnp.split(sending, lax.axis_size(('face', 'sub')...  14.5 us
    dot_general x3, matrix products, finish(): branch = jnp.dot(hidden, w_out, preferred_element_type=jnp.float32)  11.5 us
    all_to_all x1, starting transfers between devices, sum_at_owner(): lax.all_to_all(parts, axis, split_axis=0, concat_axis=0, tiled=True)  9.42 us
    all_to_all x1, starting transfers between devices, shards(): lax.all_to_all(jnp.stack(jnp.split(sending, lax.axis_size(('face', 'sub')...  7.84 us
    ppermute x3, starting transfers between devices, extended_2(): lax.ppermute(lax.slice_in_dim(block, 0, width, axis=dim), axis, backward)  7.53 us
  transfers between devices with their start and end apart: 10, of which 7 were waited for; matrix products, arithmetic and copies ran while one was open for 2% of the time, Pallas kernels for 0%

profile of v1, /device:TPU:1, one launch (start us, length us, event | category | flops | bytes accessed | tf_op | source)
XLA Modules:
  0.0 240.0 jit_solution(4553650336770166513)
XLA Ops:
  0.0 1.1 fusion.90
  2.1 9.4 %all-to-all-start = ((bf16[32,4,6,256]{3,1,2,0:T(4,128)(2,1)}), bf16[32,4,6,256]{3,1,2,0:T(4,128)(2,1)S(1)}, u32[]{:S(2)}, u32[]{:S(2)}) async-start(bf16[32,4,6,256]{3,1,2,0:T(4,128)(2,1)} %copy.433), calls=%async_computation | async-start | bytes 786432 | tf_op jit(solution)/shard_map/all_to_all | solution.py:32
  11.6 2.8 %collective-permute-start.3 = (bf16[1,4,256]{2,1,0:T(4,128)(2,1)S(1)}, bf16[1,4,256]{2,1,0:T(4,128)(2,1)S(1)}, u32[]{:S(2)}, u32[]{:S(2)}) collective-permute-start(bf16[1,4,256]{2,1,0:T(4,128)(2,1)S(1)} %bitcast.714), channel_id=1, source_target_pairs={{32,0},{64,32},{96,64},{0,96},{33,1},{65,33},{97,65},{1,97},{34,2}... | collective-permute-start | bytes 6152 | tf_op jit(solution)/shard_map/ppermute | solution.py:20
  15.7 6.1 %all-to-all-done = bf16[32,4,6,256]{3,1,2,0:T(4,128)(2,1)S(1)} async-done(((bf16[32,4,6,256]{3,1,2,0:T(4,128)(2,1)}), bf16[32,4,6,256]{3,1,2,0:T(4,128)(2,1)S(1)}, u32[]{:S(2)}, u32[]{:S(2)}) %all-to-all-start) | async-done | bytes 393248 | tf_op jit(solution)/shard_map/all_to_all | solution.py:32
  22.0 2.8 %collective-permute-start = (bf16[3,4,256]{2,1,0:T(4,128)(2,1)S(1)}, bf16[3,4,256]{2,1,0:T(4,128)(2,1)S(1)}, u32[]{:S(2)}, u32[]{:S(2)}) collective-permute-start(bf16[3,4,256]{2,1,0:T(4,128)(2,1)S(1)} %pad_maximum_fusion.10), channel_id=1, source_target_pairs={{32,0},{64,32},{96,64},{0,96},{33,1},{65,33},{97,65},{1,97},{34,2}... | collective-permute-start | bytes 18440 | tf_op jit(solution)/shard_map/ppermute | solution.py:20
  25.6 3.0 %collective-permute-done.1 = bf16[3,4,256]{2,1,0:T(4,128)(2,1)S(1)} collective-permute-done((bf16[3,4,256]{2,1,0:T(4,128)(2,1)S(1)}, bf16[3,4,256]{2,1,0:T(4,128)(2,1)S(1)}, u32[]{:S(2)}, u32[]{:S(2)}) %collective-permute-start.1) | collective-permute-done | bytes 6176 | tf_op jit(solution)/shard_map/ppermute | solution.py:17
  29.5 5.0 %all-to-all-start.1 = ((bf16[32,6,4,256]{3,2,1,0:T(4,128)(2,1)}), bf16[32,6,4,256]{3,2,1,0:T(4,128)(2,1)S(1)}, u32[]{:S(2)}, u32[]{:S(2)}) async-start(bf16[32,6,4,256]{3,2,1,0:T(4,128)(2,1)} %broadcast_in_dim.92), calls=%async_computation.1 | async-start | bytes 786432 | tf_op jit(solution)/shard_map/all_to_all | solution.py:44
  34.8 3.5 %collective-permute-start.4 = (bf16[3,1,130,256]{3,2,1,0:T(8,128)(2,1)S(1)}, bf16[3,1,130,256]{3,2,1,0:T(8,128)(2,1)S(1)}, u32[]{:S(2)}, u32[]{:S(2)}) collective-permute-start(bf16[3,1,130,256]{3,2,1,0:T(8,128)(2,1)S(1)} %get-tuple-element.166), channel_id=1, source_target_pairs={{0,1},{1,2},{2,3},{3,4},{4,5},{5,6},{6,7},{7,8},{8,9},{9,10},{10,1... | collective-permute-start | bytes 599048 | tf_op jit(solution)/shard_map/ppermute | solution.py:17
  38.4 1.9 collective-permute-start.5
  40.3 4.5 %all-to-all-done.1 = bf16[32,6,4,256]{3,2,1,0:T(4,128)(2,1)S(1)} async-done(((bf16[32,6,4,256]{3,2,1,0:T(4,128)(2,1)}), bf16[32,6,4,256]{3,2,1,0:T(4,128)(2,1)S(1)}, u32[]{:S(2)}, u32[]{:S(2)}) %all-to-all-start.1) | async-done | bytes 393248 | tf_op jit(solution)/shard_map/all_to_all | solution.py:44
  46.5 2.2 fusion.86
  49.4 2.8 %gather_fusion = bf16[512,3,256]{2,1,0:T(4,128)(2,1)S(1)} fusion(bf16[4,3,128,256]{3,1,2,0:T(4,128)(2,1)S(1)} %copy.442, s32[512]{0:T(512)S(1)} %fusion.195), kind=kCustom, calls=%fused_computation.clone | custom fusion | bytes 1576960 | tf_op jit(solution)/shard_map/vmap(jit(_take))/gather | solution.py:78
  129.5 7.8 %all-to-all-start.2 = ((bf16[128,3,4,1,1,256]{5,2,1,4,3,0:T(4,128)(2,1)}), bf16[128,3,4,1,1,256]{5,2,1,4,3,0:T(4,128)(2,1)S(1)}, u32[]{:S(2)}, u32[]{:S(2)}) async-start(bf16[128,3,4,1,1,256]{5,2,1,4,3,0:T(4,128)(2,1)} %constant_dynamic-update-slice_fusion.6), calls=%async_computation.2 | async-start | bytes 1572864 | tf_op jit(solution)/shard_map/all_to_all | solution.py:152
  137.3 1.6 compare_and_fusion.5
  139.0 14.5 %all-to-all-done.2 = bf16[128,3,4,1,1,256]{5,2,1,4,3,0:T(4,128)(2,1)S(1)} async-done(((bf16[128,3,4,1,1,256]{5,2,1,4,3,0:T(4,128)(2,1)}), bf16[128,3,4,1,1,256]{5,2,1,4,3,0:T(4,128)(2,1)S(1)}, u32[]{:S(2)}, u32[]{:S(2)}) %all-to-all-start.2) | async-done | bytes 786464 | tf_op jit(solution)/shard_map/all_to_all | solution.py:152
  153.7 5.4 %gather_fusion.2 = bf16[1536,256]{1,0:T(8,128)(2,1)} fusion(bf16[1536,256]{1,0:T(8,128)(2,1)S(1)} %bitcast.666, s32[2048]{0:T(1024)S(1)} %get-tuple-element.219), kind=kCustom, calls=%fused_computation.3.clone | custom fusion | bytes 1579008 | tf_op jit(solution)/shard_map/jit(_take)/gather | solution.py:185
  159.0 5.3 %gather_fusion.3 = bf16[1536,256]{1,0:T(8,128)(2,1)} fusion(bf16[1536,256]{1,0:T(8,128)(2,1)S(1)} %bitcast.667, s32[2048]{0:T(1024)S(1)} %get-tuple-element.218), kind=kCustom, calls=%fused_computation.4.clone | custom fusion | bytes 1579008 | tf_op jit(solution)/shard_map/jit(_take)/gather | solution.py:185
  164.4 5.4 %gather_fusion.4 = bf16[1536,256]{1,0:T(8,128)(2,1)} fusion(bf16[1536,256]{1,0:T(8,128)(2,1)S(1)} %bitcast.668, s32[2048]{0:T(1024)S(1)} %get-tuple-element.217), kind=kCustom, calls=%fused_computation.5.clone | custom fusion | bytes 1579008 | tf_op jit(solution)/shard_map/jit(_take)/gather | solution.py:185
  169.7 5.3 %gather_fusion.5 = bf16[1536,256]{1,0:T(8,128)(2,1)} fusion(bf16[1536,256]{1,0:T(8,128)(2,1)S(1)} %bitcast.669, s32[2048]{0:T(1024)S(1)} %get-tuple-element.216), kind=kCustom, calls=%fused_computation.6.clone | custom fusion | bytes 1579008 | tf_op jit(solution)/shard_map/jit(_take)/gather | solution.py:185
  175.1 5.4 %gather_fusion.6 = bf16[1536,256]{1,0:T(8,128)(2,1)} fusion(bf16[1536,256]{1,0:T(8,128)(2,1)S(1)} %bitcast.670, s32[2048]{0:T(1024)S(1)} %get-tuple-element.215), kind=kCustom, calls=%fused_computation.7.clone | custom fusion | bytes 1579008 | tf_op jit(solution)/shard_map/jit(_take)/gather | solution.py:185
  180.4 4.8 %gather_fusion.1 = bf16[1536,256]{1,0:T(8,128)(2,1)S(1)} fusion(bf16[1536,256]{1,0:T(8,128)(2,1)S(1)} %bitcast.671, s32[2048]{0:T(1024)S(1)} %pad_clamp_fusion.6), kind=kCustom, calls=%fused_computation.1.clone | custom fusion | bytes 1579008 | tf_op jit(solution)/shard_map/jit(_take)/gather | solution.py:185
  185.2 4.8 %gather_fusion.7 = bf16[1536,256]{1,0:T(8,128)(2,1)S(1)} fusion(bf16[1536,256]{1,0:T(8,128)(2,1)S(1)} %bitcast.672, s32[2048]{0:T(1024)S(1)} %get-tuple-element.214), kind=kCustom, calls=%fused_computation.8.clone | custom fusion | bytes 1579008 | tf_op jit(solution)/shard_map/jit(_take)/gather | solution.py:185
  190.0 1.5 broadcast_select_fusion.5
  195.3 1.2 fusion.77
  196.4 1.5 copy.445
  197.9 4.7 %all-to-all-start.3 = ((bf16[3,4,1,128,256]{4,1,2,0,3:T(4,128)(2,1)}), bf16[3,4,1,128,256]{4,1,2,0,3:T(4,128)(2,1)S(1)}, u32[]{:S(2)}, u32[]{:S(2)}) async-start(bf16[3,4,1,128,256]{4,1,2,0,3:T(4,128)(2,1)} %copy.445), calls=%async_computation.3 | async-start | bytes 1572864 | tf_op jit(solution)/shard_map/all_to_all | solution.py:188
  202.7 16.4 %all-to-all-done.3 = bf16[3,4,1,128,256]{4,1,2,0,3:T(4,128)(2,1)S(1)} async-done(((bf16[3,4,1,128,256]{4,1,2,0,3:T(4,128)(2,1)}), bf16[3,4,1,128,256]{4,1,2,0,3:T(4,128)(2,1)S(1)}, u32[]{:S(2)}, u32[]{:S(2)}) %all-to-all-start.3) | async-done | bytes 786464 | tf_op jit(solution)/shard_map/all_to_all | solution.py:188
  219.4 2.8 %gather_fusion.8 = bf16[512,3,256]{2,1,0:T(4,128)(2,1)S(1)} fusion(bf16[4,3,128,256]{3,1,2,0:T(4,128)(2,1)S(1)} %bitcast.682, s32[512]{0:T(512)S(1)} %fusion.195), kind=kCustom, calls=%fused_computation.2.clone | custom fusion | bytes 1576960 | tf_op jit(solution)/shard_map/vmap(jit(_take))/gather | solution.py:78
  222.9 17.1 %while.10 = (s32[]{:T(128)}, bf16[3,4,128,256]{3,2,1,0:T(8,128)(2,1)}, bf16[3,4,128,256]{3,2,1,0:T(8,128)(2,1)S(1)}, f32[256]{0:T(256)S(1)}, bf16[3,4,128,256]{3...) while((s32[]{:T(128)}, ...), condition=%wide.region_4.7_spmd, body=%wide.region_1.6_spmd.sunk | while | flops 430178816 | bytes 6838949 | solution.py:211
  224.1 3.8 %fusion.214 = bf16[512,256]{1,0:T(8,128)(2,1)S(1)} fusion(bf16[768,256]{1,0:T(8,128)(2,1)S(1)} %copy-done.11, bf16[512,256]{1,0:T(8,128)(2,1)S(1)} %fusion.213, bf16[256,768]{1,0:T(8,128)(2,1)S(1)} %copy-done.10, bf16[512,256]{1,0:T(8,128)(2,1)S(1)} %bitcast.680, f32[256]{0:T(256)S(1)} %get-tuple-element.294), kind=kOutput, calls=%fused_computation.30.clone.1 | convolution fusion | flops 428736512 | bytes 1573888 | tf_op jit(solution)/shard_map/while/body/eval_jaxpr/dot_general | solution.py:206
  229.7 3.8 %fusion.214 = bf16[512,256]{1,0:T(8,128)(2,1)S(1)} fusion(bf16[768,256]{1,0:T(8,128)(2,1)S(1)} %copy-done.11, bf16[512,256]{1,0:T(8,128)(2,1)S(1)} %fusion.213, bf16[256,768]{1,0:T(8,128)(2,1)S(1)} %copy-done.10, bf16[512,256]{1,0:T(8,128)(2,1)S(1)} %bitcast.680, f32[256]{0:T(256)S(1)} %get-tuple-element.294), kind=kOutput, calls=%fused_computation.30.clone.1 | convolution fusion | flops 428736512 | bytes 1573888 | tf_op jit(solution)/shard_map/while/body/eval_jaxpr/dot_general | solution.py:206
  235.4 3.8 %fusion.214 = bf16[512,256]{1,0:T(8,128)(2,1)S(1)} fusion(bf16[768,256]{1,0:T(8,128)(2,1)S(1)} %copy-done.11, bf16[512,256]{1,0:T(8,128)(2,1)S(1)} %fusion.213, bf16[256,768]{1,0:T(8,128)(2,1)S(1)} %copy-done.10, bf16[512,256]{1,0:T(8,128)(2,1)S(1)} %bitcast.680, f32[256]{0:T(256)S(1)} %get-tuple-element.294), kind=kOutput, calls=%fused_computation.30.clone.1 | convolution fusion | flops 428736512 | bytes 1573888 | tf_op jit(solution)/shard_map/while/body/eval_jaxpr/dot_general | solution.py:206
  (260 shorter events, 94.4 us)
Async XLA Ops:
  1.1 10.4 %copy-start = (bf16[3,1,4,128,256]{4,3,2,1,0:T(8,128)(2,1)S(1)}, bf16[3,1,4,128,256]{4,3,2,1,0:T(8,128)(2,1)}, u32[]{:S(2)}) copy-start(bf16[3,1,4,128,256]{4,3,2,1,0:T(8,128)(2,1)} %param.15) | copy-start | bytes 2359300
  1.1 13.4 %copy-start.7 = (f32[9,256]{1,0:T(8,128)S(1)}, f32[9,256]{1,0:T(8,128)}, u32[]{:S(2)}) copy-start(f32[9,256]{1,0:T(8,128)} %param.16) | copy-start | bytes 27652
  2.1 19.7 %all-to-all-start = ((bf16[32,4,6,256]{3,1,2,0:T(4,128)(2,1)}), bf16[32,4,6,256]{3,1,2,0:T(4,128)(2,1)S(1)}, u32[]{:S(2)}, u32[]{:S(2)}) async-start(bf16[32,4,6,256]{3,1,2,0:T(4,128)(2,1)} %copy.433), calls=%async_computation | async-start | bytes 786432 | tf_op jit(solution)/shard_map/all_to_all | solution.py:32
  11.6 23.0 %collective-permute-start.3 = (bf16[1,4,256]{2,1,0:T(4,128)(2,1)S(1)}, bf16[1,4,256]{2,1,0:T(4,128)(2,1)S(1)}, u32[]{:S(2)}, u32[]{:S(2)}) collective-permute-start(bf16[1,4,256]{2,1,0:T(4,128)(2,1)S(1)} %bitcast.714), channel_id=1, source_target_pairs={{32,0},{64,32},{96,64},{0,96},{33,1},{65,33},{97,65},{1,97},{34,2}... | collective-permute-start | bytes 6152 | tf_op jit(solution)/shard_map/ppermute | solution.py:20
  14.4 20.3 %collective-permute-start.2 = (bf16[1,4,256]{2,1,0:T(4,128)(2,1)S(1)}, bf16[1,4,256]{2,1,0:T(4,128)(2,1)S(1)}, u32[]{:S(2)}, u32[]{:S(2)}) collective-permute-start(bf16[1,4,256]{2,1,0:T(4,128)(2,1)S(1)} %bitcast.713), channel_id=1, source_target_pairs={{0,32},{32,64},{64,96},{96,0},{1,33},{33,65},{65,97},{97,1},{2,34}... | collective-permute-start | bytes 6152 | tf_op jit(solution)/shard_map/ppermute | solution.py:17
  22.0 3.6 %collective-permute-start = (bf16[3,4,256]{2,1,0:T(4,128)(2,1)S(1)}, bf16[3,4,256]{2,1,0:T(4,128)(2,1)S(1)}, u32[]{:S(2)}, u32[]{:S(2)}) collective-permute-start(bf16[3,4,256]{2,1,0:T(4,128)(2,1)S(1)} %pad_maximum_fusion.10), channel_id=1, source_target_pairs={{32,0},{64,32},{96,64},{0,96},{33,1},{65,33},{97,65},{1,97},{34,2}... | collective-permute-start | bytes 18440 | tf_op jit(solution)/shard_map/ppermute | solution.py:20
  24.8 3.8 %collective-permute-start.1 = (bf16[3,4,256]{2,1,0:T(4,128)(2,1)S(1)}, bf16[3,4,256]{2,1,0:T(4,128)(2,1)S(1)}, u32[]{:S(2)}, u32[]{:S(2)}) collective-permute-start(bf16[3,4,256]{2,1,0:T(4,128)(2,1)S(1)} %pad_maximum_fusion.11), channel_id=1, source_target_pairs={{0,32},{32,64},{64,96},{96,0},{1,33},{33,65},{65,97},{97,1},{2,34}... | collective-permute-start | bytes 18440 | tf_op jit(solution)/shard_map/ppermute | solution.py:17
  29.5 15.3 %all-to-all-start.1 = ((bf16[32,6,4,256]{3,2,1,0:T(4,128)(2,1)}), bf16[32,6,4,256]{3,2,1,0:T(4,128)(2,1)S(1)}, u32[]{:S(2)}, u32[]{:S(2)}) async-start(bf16[32,6,4,256]{3,2,1,0:T(4,128)(2,1)} %broadcast_in_dim.92), calls=%async_computation.1 | async-start | bytes 786432 | tf_op jit(solution)/shard_map/all_to_all | solution.py:44
  34.8 10.3 %collective-permute-start.4 = (bf16[3,1,130,256]{3,2,1,0:T(8,128)(2,1)S(1)}, bf16[3,1,130,256]{3,2,1,0:T(8,128)(2,1)S(1)}, u32[]{:S(2)}, u32[]{:S(2)}) collective-permute-start(bf16[3,1,130,256]{3,2,1,0:T(8,128)(2,1)S(1)} %get-tuple-element.166), channel_id=1, source_target_pairs={{0,1},{1,2},{2,3},{3,4},{4,5},{5,6},{6,7},{7,8},{8,9},{9,10},{10,1... | collective-permute-start | bytes 599048 | tf_op jit(solution)/shard_map/ppermute | solution.py:17
  38.4 7.2 %collective-permute-start.5 = (bf16[3,1,130,256]{3,2,1,0:T(8,128)(2,1)S(1)}, bf16[3,1,130,256]{3,2,1,0:T(8,128)(2,1)S(1)}, u32[]{:S(2)}, u32[]{:S(2)}) collective-permute-start(bf16[3,1,130,256]{3,2,1,0:T(8,128)(2,1)S(1)} %get-tuple-element.167), channel_id=1, source_target_pairs={{1,0},{2,1},{3,2},{4,3},{5,4},{6,5},{7,6},{8,7},{9,8},{10,9},{11,1... | collective-permute-start | bytes 599048 | tf_op jit(solution)/shard_map/ppermute | solution.py:20
  45.8 0.7 copy-start.8
  113.3 25.7 %copy-start.6 = (f32[7,256]{1,0:T(8,128)S(1)}, f32[7,256]{1,0:T(8,128)}, u32[]{:S(2)}) copy-start(f32[7,256]{1,0:T(8,128)} %param.18) | copy-start | bytes 21508
  129.5 24.1 %all-to-all-start.2 = ((bf16[128,3,4,1,1,256]{5,2,1,4,3,0:T(4,128)(2,1)}), bf16[128,3,4,1,1,256]{5,2,1,4,3,0:T(4,128)(2,1)S(1)}, u32[]{:S(2)}, u32[]{:S(2)}) async-start(bf16[128,3,4,1,1,256]{5,2,1,4,3,0:T(4,128)(2,1)} %constant_dynamic-update-slice_fusion.6), calls=%async_computation.2 | async-start | bytes 1572864 | tf_op jit(solution)/shard_map/all_to_all | solution.py:152
  190.0 1.5 copy-start.4
  191.5 1.1 copy-start.2
  191.8 1.2 copy-start.3
  192.9 1.2 copy-start.1
  194.6 0.7 copy-start.9
  197.9 21.1 %all-to-all-start.3 = ((bf16[3,4,1,128,256]{4,1,2,0,3:T(4,128)(2,1)}), bf16[3,4,1,128,256]{4,1,2,0,3:T(4,128)(2,1)S(1)}, u32[]{:S(2)}, u32[]{:S(2)}) async-start(bf16[3,4,1,128,256]{4,1,2,0,3:T(4,128)(2,1)} %copy.445), calls=%async_computation.3 | async-start | bytes 1572864 | tf_op jit(solution)/shard_map/all_to_all | solution.py:188
  222.2 0.7 copy-start.5
  222.2 0.7 copy-start.12
  222.9 1.0 copy-start.10
  222.9 1.1 copy-start.11
  228.6 1.0 copy-start.10
  228.6 1.1 copy-start.11
  234.3 1.0 copy-start.10
  234.3 1.1 copy-start.11
